TPU v7x, 32 devices: a whole 2x2x4 slice. The times are simulated.
32 devices in a mesh: row: 4 (over y, core), col: 8 (over z, x).
Axes of the slice: x: 2, y: 2, z: 4, core: 2. Of those that a mesh axis runs over, the one named last changes fastest.
Arguments:
- stored: float32 [40, 4, 128, 20, 8, 128], P(None, 'row', None, None, 'col'), may hold values from -1 to 13
- rhs: float32 [20, 8, 128, 128], P(None, 'col'), may hold values from -60 to 60
Outputs:
- solution: float32 [20, 8, 128, 128], P(None, 'col')
- residual: float32 [20, 8, 128, 128], P(None, 'col')
All inputs are finite; a program needn't handle non-finite values.
Results may differ from a plain program's by a relative error of at most 0.0003.
Values sent between devices are 32-bit elements; how exact they have to be, the bound alone decides.
No kernel may reach another device: no remote copies, remote signals or barrier semaphores. Data moves between devices by JAX's collectives and lax.ppermute only.
A program may use at most 192 MiB of HBM per device.

v0:
```python
import jax
import jax.numpy as jnp
from jax import lax
from jax.sharding import PartitionSpec as P

ITERS = 2
HIGHEST = lax.Precision.HIGHEST


def partner_2(value, axis, distance):
    mask = 2**distance
    pairs = [(source, source ^ mask) for source in range(lax.axis_size(axis))]
    return lax.ppermute(value, axis, pairs)


def spread(value, axis, source):
    kept = jnp.where(lax.axis_index(axis) == source, value, 0).astype(value.dtype)
    return lax.psum(kept, axis)


def gram_local(left_side, right_side):
    columns_n = left_side.shape[-1]
    return jnp.einsum(
        "nk,nl->kl",
        left_side.reshape(-1, columns_n),
        right_side.reshape(-1, columns_n),
        precision=HIGHEST,
        preferred_element_type=jnp.float32,
    )


def mix_right(vectors, matrix):
    columns_n = vectors.shape[-1]
    return jnp.dot(
        vectors.reshape(-1, columns_n),
        matrix,
        precision=HIGHEST,
        preferred_element_type=jnp.float32,
    ).reshape(vectors.shape)


def solve_spd(matrix, target):
    factor = jnp.linalg.cholesky(matrix)
    return jax.scipy.linalg.cho_solve((factor, True), target)


def to_rowset(column_set, row_index, col_index):
    low_bits = lax.axis_size("row").bit_length() - 1
    high_bits = lax.axis_size("col").bit_length() - 1
    current = column_set
    for bit_pos in range(low_bits):
        partner = partner_2(current, "col", bit_pos)
        differs = col_index >> bit_pos & 1 != row_index >> bit_pos & 1
        current = jnp.where(differs, partner, current)
    joined = current[:, None]
    for bit_pos in range(low_bits, high_bits):
        partner = partner_2(joined, "col", bit_pos)
        lower_half = col_index >> bit_pos & 1 == 0
        joined = jnp.where(
            lower_half,
            jnp.concatenate([joined, partner], axis=1),
            jnp.concatenate([partner, joined], axis=1),
        )
    return joined.reshape((-1,) + column_set.shape[1:])


def to_colset(row_set, col_index):
    rows_n = lax.axis_size("row")
    groups = lax.axis_size("col") // rows_n
    shape_in = row_set.shape
    regrouped = row_set.reshape(shape_in[:-3] + (shape_in[-3] // groups, groups) + shape_in[-2:])
    selected = lax.dynamic_index_in_dim(
        regrouped, col_index // rows_n, regrouped.ndim - 3, keepdims=False
    )
    return spread(selected, "row", col_index % rows_n)


def local_products(lower_part, column_set, row_set):
    columns_n = column_set.shape[-1]
    by_rows = jnp.dot(
        lower_part,
        column_set.reshape(-1, columns_n),
        precision=HIGHEST,
        preferred_element_type=jnp.float32,
    )
    by_columns = jnp.einsum(
        "nm,nk->mk",
        lower_part,
        row_set.reshape(-1, columns_n),
        precision=HIGHEST,
        preferred_element_type=jnp.float32,
    )
    return (by_rows, by_columns)


def columns_whole(by_columns, shape_out):
    return lax.psum(by_columns, "row").reshape(shape_out)


def rows_whole(by_rows, shape_out):
    return lax.psum(by_rows, "col").reshape(shape_out)


def per_device(stored, rhs):
    row_index = lax.axis_index("row")
    col_index = lax.axis_index("col")
    rows_n = lax.axis_size("row")
    cols_n = lax.axis_size("col")
    row_blocks = stored.shape[0]
    block_size = stored.shape[2]
    col_blocks = stored.shape[3]
    columns_n = rhs.shape[-1]
    block_rows = jnp.arange(row_blocks, dtype=jnp.int32) * rows_n + row_index
    block_cols = jnp.arange(col_blocks, dtype=jnp.int32) * cols_n + col_index
    weight = jnp.where(
        block_rows[:, None] > block_cols[None, :],
        1.0,
        jnp.where(block_rows[:, None] == block_cols[None, :], 0.5, 0.0),
    ).astype(jnp.float32)
    lower_part = (
        stored.reshape(row_blocks, block_size, col_blocks, block_size) * weight[:, None, :, None]
    ).reshape(row_blocks * block_size, col_blocks * block_size)
    start_set = rhs.reshape(col_blocks, block_size, columns_n)

    def reduce_grams(stacked):
        return lax.psum(stacked, "col")

    solution = jnp.zeros_like(start_set)
    residual = start_set
    direction = start_set
    gram_now = reduce_grams(gram_local(residual, residual)[None])[0]
    for iteration in range(ITERS):
        row_set = to_rowset(direction, row_index, col_index)
        by_rows, by_columns = local_products(lower_part, direction, row_set)
        column_part = columns_whole(by_columns, direction.shape)
        row_piece = to_colset(rows_whole(by_rows, row_set.shape), col_index)
        applied = column_part + row_piece
        last_turn = iteration + 1 == ITERS
        gram_sums = reduce_grams(gram_local(direction, applied)[None])
        curvature = gram_sums[0]
        step_size = solve_spd(curvature, gram_now)
        solution = solution + mix_right(direction, step_size)
        residual = residual - mix_right(applied, step_size)
        if not last_turn:
            gram_next = reduce_grams(gram_local(residual, residual)[None])[0]
            mix_factor = solve_spd(gram_now, gram_next)
            direction = residual + mix_right(direction, mix_factor)
            gram_now = gram_next
    final_pair = (solution, residual)
    return (final_pair[0].reshape(rhs.shape), final_pair[1].reshape(rhs.shape))


def solution(mesh):
    placed = (P(None, "row", None, None, "col", None), P(None, "col", None, None))
    return jax.shard_map(
        per_device,
        mesh=mesh,
        in_specs=placed,
        out_specs=(P(None, "col", None, None), P(None, "col", None, None)),
        check_vma=False,
    )
```

profile of v0, /device:TPU:0, one launch (start us, length us, event | category | flops | bytes accessed | tf_op | source)
XLA Modules:
  0.0 1001.4 jit_solution(6003752556516424082)
XLA Ops:
  7.2 3.0 collective-permute-start
  10.3 28.9 %collective-permute-done = f32[20,128,128]{2,1,0:T(8,128)S(1)} collective-permute-done((f32[20,128,128]{2,1,0:T(8,128)}, f32[20,128,128]{2,1,0:T(8,128)S(1)}, u32[]{:S(2)}, u32[]{:S(2)}) %collective-permute-start) | collective-permute-done | bytes 1310752 | tf_op jit(solution)/shard_map/ppermute | solution.py:13
  39.2 1.5 broadcast_select_fusion.1
  40.7 1.9 collective-permute-start.1
  42.6 163.2 %multiply_reduce_fusion = f32[40,128,20,128]{3,2,1,0:T(8,128)} fusion(f32[40,1,128,20,1,128]{5,4,3,2,1,0:T(1,128)} %param.5, f32[40,20]{1,0:T(8,128)S(1)} %select_select_fusion.3), kind=kLoop, calls=%fused_computation.8 | loop fusion | flops 13107200 | bytes 104860800 | tf_op jit(solution)/shard_map/mul | solution.py:121
  205.8 1.2 select_bitcast_fusion.1
  207.0 2.6 collective-permute-start.2
  209.6 52.8 %fusion.4 = f32[5120,128]{1,0:T(8,128)S(1)} fusion(f32[2560,128]{1,0:T(8,128)S(1)} %bitcast.123, f32[640,8,20,128]{3,2,1,0:T(8,128)} %bitcast.118), kind=kOutput, calls=%fused_computation.4 | convolution fusion | flops 20132659200 | bytes 56360960 | tf_op jit(solution)/shard_map/dot_general | solution.py:80
  262.5 1.7 copy.18
  264.2 1.4 collective-permute-done.2
  265.6 2.0 maximum_select_fusion
  267.8 106.5 %fusion.6 = f32[2560,128]{1,0:T(8,128)S(1)} fusion(f32[5120,128]{1,0:T(8,128)S(1)} %bitcast.129, f32[640,8,20,128]{3,2,1,0:T(8,128)} %bitcast.119), kind=kOutput, calls=%fused_computation.6 | convolution fusion | flops 20132659200 | bytes 56360960 | tf_op jit(solution)/shard_map/nm,nk->mk/dot_general | solution.py:86
  374.4 5.6 all-reduce.9.cloned.1.call-done
  380.0 2.5 bitcast_add_fusion.1
  382.6 2.9 convolution_bitcast_fusion.5
  385.4 35.7 %all-reduce.17.cloned.1.call-done = f32[20,128,128]{2,1,0:T(8,128)} async-done(((f32[20,128,128]{2,1,0:T(8,128)}), f32[20,128,128]{2,1,0:T(8,128)}) %all-reduce.17.cloned.1.call-update) | async-done | bytes 1310736 | tf_op jit(solution)/shard_map/psum | solution.py:97
  421.1 4.2 convolution_bitcast_fusion.6
  425.3 70.8 %all-reduce.21.cloned.1.call-done = (f32[128,128]{0,1:T(8,128)}, f32[128,128]{0,1:T(8,128)}) async-done(((f32[128,128]{0,1:T(8,128)}, f32[128,128]{0,1:T(8,128)}), (f32[128,128]{0,1:T(8,128)}, f32[128,128]{0,1:T(8,128)})) %all-reduce.21.cloned.1.call-update) | async-done | bytes 131088 | tf_op jit(solution)/shard_map/psum | solution.py:126
  496.1 0.9 copy.19
  497.1 0.9 copy.23
  498.0 0.9 fusion.25
  498.9 11.7 %cholesky.70 = f32[128,128]{1,0:T(8,128)S(1)} custom-call(f32[128,128]{1,0:T(8,128)S(1)} %get-tuple-element.10), custom_call_target="Cholesky" | custom-call | tf_op jit(solution)/shard_map/jit(cholesky)/cholesky | solution.py:43
  510.6 0.6 compare_reduce_fusion.1
  511.3 11.7 %cholesky.59 = f32[128,128]{1,0:T(8,128)S(1)} custom-call(f32[128,128]{1,0:T(8,128)S(1)} %get-tuple-element.11), custom_call_target="Cholesky" | custom-call | tf_op jit(solution)/shard_map/jit(cholesky)/cholesky | solution.py:43
  523.0 0.6 compare_reduce_fusion.2
  523.7 0.7 fusion.14
  524.3 9.8 custom-call.9
  534.2 1.1 fusion.29
  535.5 2.5 convolution_subtract_fusion.1
  538.0 3.3 convolution_bitcast_fusion.4
  541.3 0.7 fusion.15
  542.0 9.8 custom-call.10
  551.8 58.1 %all-reduce.11.cloned.1.call-done = f32[128,128]{1,0:T(8,128)} async-done(((f32[128,128]{1,0:T(8,128)}), f32[128,128]{1,0:T(8,128)}) %all-reduce.11.cloned.1.call-update) | async-done | bytes 65552 | tf_op jit(solution)/shard_map/psum | solution.py:126
  609.9 1.1 fusion.23
  611.2 2.4 convolution_bitcast_fusion
  613.6 2.8 copy.25
  616.3 1.5 add.81
  617.8 1.5 collective-permute-start.3
  619.3 27.2 %collective-permute-done.3 = f32[20,128,128]{2,1,0:T(8,128)S(1)} collective-permute-done((f32[20,128,128]{2,1,0:T(8,128)S(1)}, f32[20,128,128]{2,1,0:T(8,128)S(1)}, u32[]{:S(2)}, u32[]{:S(2)}) %collective-permute-start.3) | collective-permute-done | bytes 1310752 | tf_op jit(solution)/shard_map/ppermute | solution.py:13
  646.7 1.6 collective-permute-start.4
  648.3 26.3 %collective-permute-done.4 = f32[20,128,128]{2,1,0:T(8,128)S(1)} collective-permute-done((f32[20,128,128]{2,1,0:T(8,128)S(1)}, f32[20,128,128]{2,1,0:T(8,128)S(1)}, u32[]{:S(2)}, u32[]{:S(2)}) %collective-permute-start.4) | collective-permute-done | bytes 1310752 | tf_op jit(solution)/shard_map/ppermute | solution.py:13
  674.6 1.2 select_bitcast_fusion
  675.8 2.0 collective-permute-start.5
  677.7 52.8 %fusion = f32[5120,128]{1,0:T(8,128)S(1)} fusion(f32[2560,128]{1,0:T(8,128)S(1)} %bitcast.127, f32[640,8,20,128]{3,2,1,0:T(8,128)} %bitcast.120), kind=kOutput, calls=%fused_computation | convolution fusion | flops 20132659200 | bytes 56360960 | tf_op jit(solution)/shard_map/dot_general | solution.py:80
  730.6 1.7 copy.27
  732.3 3.0 maximum_select_fusion.1
  735.3 0.3 copy.26
  735.6 95.9 %fusion.2 = f32[2560,128]{1,0:T(8,128)} fusion(f32[5120,128]{1,0:T(8,128)S(1)} %bitcast.128, f32[640,8,20,128]{3,2,1,0:T(8,128)} %bitcast.121), kind=kOutput, calls=%fused_computation.2 | convolution fusion | flops 20132659200 | bytes 56360960 | tf_op jit(solution)/shard_map/nm,nk->mk/dot_general | solution.py:86
  831.4 16.4 %all-reduce.13.cloned.1.call-done = f32[20,2,128,128]{3,2,0,1:T(8,128)} async-done(((f32[20,2,128,128]{3,2,0,1:T(8,128)}), f32[20,2,128,128]{3,2,0,1:T(8,128)}) %all-reduce.13.cloned.1.call-update) | async-done | bytes 2621456 | tf_op jit(solution)/shard_map/psum | solution.py:101
  847.8 2.9 bitcast_add_fusion
  850.8 38.2 %all-reduce.19.cloned.1.call-done = f32[20,128,128]{2,1,0:T(8,128)} async-done(((f32[20,128,128]{2,1,0:T(8,128)}), f32[20,128,128]{2,1,0:T(8,128)}) %all-reduce.19.cloned.1.call-update) | async-done | bytes 1310736 | tf_op jit(solution)/shard_map/psum | solution.py:97
  889.1 4.6 convolution_bitcast_fusion.3
  893.7 2.4 convolution_bitcast_fusion.1
  896.0 2.9 copy.22
  898.9 64.2 %all-reduce.15.cloned.1.call-done = f32[128,128]{0,1:T(8,128)} async-done(((f32[128,128]{0,1:T(8,128)}), f32[128,128]{0,1:T(8,128)}) %all-reduce.15.cloned.1.call-update) | async-done | bytes 65552 | tf_op jit(solution)/shard_map/psum | solution.py:126
  963.1 0.9 copy.30
  964.0 0.9 fusion.20
  964.9 11.7 %cholesky.81 = f32[128,128]{1,0:T(8,128)S(1)} custom-call(f32[128,128]{1,0:T(8,128)S(1)} %fusion.20), custom_call_target="Cholesky" | custom-call | tf_op jit(solution)/shard_map/jit(cholesky)/cholesky | solution.py:43
  976.6 0.6 compare_reduce_fusion
  977.3 0.7 fusion.16
  977.9 9.8 custom-call.11
  987.8 0.3 fusion.18
  988.3 3.7 fusion.12
  991.9 2.2 fusion.13
  (37 shorter events, 1.6 us)
Async XLA Ops:
  7.2 372.8 %all-reduce.9.cloned.1.call-start = ((), (), s32[]{:S(2)}) async-start(), calls=%async_computation | async-start | bytes 5242880 | tf_op jit(solution)/shard_map/psum | solution.py:101
  7.2 32.0 %collective-permute-start = (f32[20,128,128]{2,1,0:T(8,128)}, f32[20,128,128]{2,1,0:T(8,128)S(1)}, u32[]{:S(2)}, u32[]{:S(2)}) collective-permute-start(f32[20,128,128]{2,1,0:T(8,128)} %bitcast.122), channel_id=1, source_target_pairs={{0,1},{1,0},{2,3},{3,2},{4,5},{5,4},{6,7},{7,6},{8,9},{9,8},{10,11... | collective-permute-start | bytes 3932168 | tf_op jit(solution)/shard_map/ppermute | solution.py:13
  40.7 165.1 %collective-permute-start.1 = (f32[20,128,128]{2,1,0:T(8,128)S(1)}, f32[20,128,128]{2,1,0:T(8,128)}, u32[]{:S(2)}, u32[]{:S(2)}) collective-permute-start(f32[20,128,128]{2,1,0:T(8,128)S(1)} %broadcast_select_fusion.1), channel_id=1, source_target_pairs={{0,2},{1,3},{2,0},{3,1},{4,6},{5,7},{6,4},{7,5},{8,10},{9,11},{10,... | collective-permute-start | bytes 3932168 | tf_op jit(solution)/shard_map/ppermute | solution.py:13
  205.8 3.8 copy-start
  207.0 58.6 %collective-permute-start.2 = (f32[20,1,128,128]{3,2,0,1:T(8,128)}, f32[20,1,128,128]{3,2,0,1:T(8,128)S(1)}, u32[]{:S(2)}, u32[]{:S(2)}) collective-permute-start(f32[20,1,128,128]{3,2,0,1:T(8,128)} %select_bitcast_fusion.1), channel_id=1, source_target_pairs={{0,4},{1,5},{2,6},{3,7},{4,0},{5,1},{6,2},{7,3},{8,12},{9,13},{10,... | collective-permute-start | bytes 3932168 | tf_op jit(solution)/shard_map/ppermute | solution.py:13
  264.2 156.9 %all-reduce.17.cloned.1.call-start = ((), (), s32[]{:S(2)}) async-start(), calls=%async_computation.4 | async-start | bytes 2621440 | tf_op jit(solution)/shard_map/psum | solution.py:97
  382.5 113.6 %all-reduce.21.cloned.1.call-start = ((), (), s32[]{:S(2)}) async-start(), calls=%async_computation.6 | async-start | bytes 262144 | tf_op jit(solution)/shard_map/psum | solution.py:126
  425.3 184.6 %all-reduce.11.cloned.1.call-start = ((), (), s32[]{:S(2)}) async-start(), calls=%async_computation.1 | async-start | bytes 131072 | tf_op jit(solution)/shard_map/psum | solution.py:126
  541.3 306.5 %all-reduce.13.cloned.1.call-start = ((), (), s32[]{:S(2)}) async-start(), calls=%async_computation.2 | async-start | bytes 5242880 | tf_op jit(solution)/shard_map/psum | solution.py:101
  617.8 59.9 %copy-start.1 = (f32[20,128,128]{2,1,0:T(8,128)}, f32[20,128,128]{2,1,0:T(8,128)S(1)}, u32[]{:S(2)}) copy-start(f32[20,128,128]{2,1,0:T(8,128)S(1)} %add.81) | copy-start | bytes 3932164
  617.8 28.7 %collective-permute-start.3 = (f32[20,128,128]{2,1,0:T(8,128)S(1)}, f32[20,128,128]{2,1,0:T(8,128)S(1)}, u32[]{:S(2)}, u32[]{:S(2)}) collective-permute-start(f32[20,128,128]{2,1,0:T(8,128)S(1)} %add.81), channel_id=1, source_target_pairs={{0,1},{1,0},{2,3},{3,2},{4,5},{5,4},{6,7},{7,6},{8,9},{9,8},{10,11... | collective-permute-start | bytes 3932168 | tf_op jit(solution)/shard_map/ppermute | solution.py:13
  646.7 27.9 %collective-permute-start.4 = (f32[20,128,128]{2,1,0:T(8,128)S(1)}, f32[20,128,128]{2,1,0:T(8,128)S(1)}, u32[]{:S(2)}, u32[]{:S(2)}) collective-permute-start(f32[20,128,128]{2,1,0:T(8,128)S(1)} %broadcast_select_fusion), channel_id=1, source_target_pairs={{0,2},{1,3},{2,0},{3,1},{4,6},{5,7},{6,4},{7,5},{8,10},{9,11},{10,... | collective-permute-start | bytes 3932168 | tf_op jit(solution)/shard_map/ppermute | solution.py:13
  675.8 56.5 %collective-permute-start.5 = (f32[20,1,128,128]{3,2,0,1:T(8,128)}, f32[20,1,128,128]{3,2,0,1:T(8,128)}, u32[]{:S(2)}, u32[]{:S(2)}) collective-permute-start(f32[20,1,128,128]{3,2,0,1:T(8,128)} %select_bitcast_fusion), channel_id=1, source_target_pairs={{0,4},{1,5},{2,6},{3,7},{4,0},{5,1},{6,2},{7,3},{8,12},{9,13},{10,... | collective-permute-start | bytes 3932168 | tf_op jit(solution)/shard_map/ppermute | solution.py:13
  732.3 156.8 %all-reduce.19.cloned.1.call-start = ((), (), s32[]{:S(2)}) async-start(), calls=%async_computation.5 | async-start | bytes 2621440 | tf_op jit(solution)/shard_map/psum | solution.py:97
  850.8 112.3 %all-reduce.15.cloned.1.call-start = ((), (), s32[]{:S(2)}) async-start(), calls=%async_computation.3 | async-start | bytes 131072 | tf_op jit(solution)/shard_map/psum | solution.py:126
  896.0 91.7 %copy-start.4 = (f32[128,128]{1,0:T(8,128)S(1)}, f32[128,128]{1,0:T(8,128)}, u32[]{:S(2)}) copy-start(f32[128,128]{1,0:T(8,128)} %all-reduce.11.cloned.1.call-done) | copy-start | bytes 196612
  896.0 92.3 %copy-start.2 = (f32[20,128,128]{2,1,0:T(8,128)S(1)}, f32[20,128,128]{2,1,0:T(8,128)}, u32[]{:S(2)}) copy-start(f32[20,128,128]{2,1,0:T(8,128)} %copy-done.1) | copy-start | bytes 3932164
  988.3 3.7 copy-start.3
Sparse Core Ops, SparseCore 0:
  264.3 115.6 all-reduce.8
  382.9 38.1 all-reduce.16
  425.4 70.6 all-reduce.20
  541.4 68.4 all-reduce.10
  732.4 115.3 all-reduce.12
  850.9 38.1 all-reduce.18
  893.8 69.2 all-reduce.14
where the time goes:
time: 1010 us; the launch traced here: 1000 us
  waiting for transfers between devices  373 us (37%)
  matrix products  339 us (34%)
  other arithmetic  250 us (25%)
  between operations  14.8 us (1%)
  starting transfers between devices  12.9 us (1%)
  local copies, waits for them, and re-layouts  12.2 us (1%)
    dot_general x2, matrix products, local_products(): jnp.einsum('nm,nk->mk', lower_part, row_set.reshape(-1, columns_n), preci...  202 us
    psum x3, waiting for transfers between devices, reduce_grams(): return lax.psum(stacked, 'col')  193 us
    mul x1, other arithmetic, per_device(): stored.reshape(row_blocks, block_size, col_blocks, block_size)  163 us
    dot_general x2, matrix products, local_products(): jnp.dot(lower_part, column_set.reshape(-1, columns_n), precision=HIGHEST,...  106 us
    ppermute x6, waiting for transfers between devices, partner_2(): return lax.ppermute(value, axis, pairs)  83.8 us
    psum x2, waiting for transfers between devices, columns_whole(): return lax.psum(by_columns, 'row').reshape(shape_out)  73.9 us
    another operation x9, other arithmetic, solve_spd(): factor = jnp.linalg.cholesky(matrix)  37.2 us
    another operation x6, other arithmetic, solve_spd(): return jax.scipy.linalg.cho_solve((factor, True), target)  31.4 us
  transfers between devices with their start and end apart: 13, of which 11 were waited for; matrix products, arithmetic and copies ran while one was open for 50% of the time, Pallas kernels for 0%

commit v1 on v0

--- a/solution.py
+++ b/solution.py
@@ -123,7 +123,7 @@
     start_set = rhs.reshape(col_blocks, block_size, columns_n)
 
     def reduce_grams(stacked):
-        return lax.psum(stacked, "col")
+        return jnp.sum(lax.all_gather(stacked, "col"), axis=0)
 
     solution = jnp.zeros_like(start_set)
     residual = start_set

time: 1010 us -> 881 us (0.87)
  waiting for transfers between devices: 373 us -> 139 us
  blocking collectives: 0 us -> 128 us
  matrix products: 339 us -> 322 us
    psum x3 -> x0, waiting for transfers between devices: 193 us -> none  [reduce_grams(): return lax.psum(stacked, 'col')]
    all_gather x0 -> x4, blocking collectives: none -> 128 us  [reduce_grams(): return jnp.sum(lax.all_gather(stacked, 'col'), axis=0)]
    psum x2, waiting for transfers between devices: 73.9 us -> 49.4 us  [columns_whole(): return lax.psum(by_columns, 'row').reshape(shape_out)]
    dot_general x2, matrix products: 202 us -> 190 us  [local_products(): jnp.einsum('nm,nk->mk', lower_part, row_set.reshape(-1, columns_n), preci...]
    ppermute x6, waiting for transfers between devices: 83.8 us -> 72.7 us  [partner_2(): return lax.ppermute(value, axis, pairs)]
  transfers between devices with their start and end apart: 13 -> 10, of which waited for: 11 -> 6; matrix products, arithmetic and copies ran while one was open for 50% -> 57% of each run, Pallas kernels for 0% -> 0%
where the time goes in v1:
time: 881 us; the launch traced here: 872 us
  matrix products  322 us (37%)
  other arithmetic  248 us (28%)
  waiting for transfers between devices  139 us (16%)
  blocking collectives  128 us (15%)
  between operations  14.5 us (2%)
  starting transfers between devices  10.6 us (1%)
  local copies, waits for them, and re-layouts  9.81 us (1%)
    dot_general x2, matrix products, local_products(): jnp.einsum('nm,nk->mk', lower_part, row_set.reshape(-1, columns_n), preci...  190 us
    mul x1, other arithmetic, per_device(): stored.reshape(row_blocks, block_size, col_blocks, block_size)  163 us
    all_gather x4, blocking collectives, reduce_grams(): return jnp.sum(lax.all_gather(stacked, 'col'), axis=0)  128 us
    dot_general x2, matrix products, local_products(): jnp.dot(lower_part, column_set.reshape(-1, columns_n), precision=HIGHEST,...  106 us
    ppermute x6, waiting for transfers between devices, partner_2(): return lax.ppermute(value, axis, pairs)  72.7 us
    psum x2, waiting for transfers between devices, columns_whole(): return lax.psum(by_columns, 'row').reshape(shape_out)  49.4 us
    another operation x9, other arithmetic, solve_spd(): factor = jnp.linalg.cholesky(matrix)  37.2 us
    another operation x6, other arithmetic, solve_spd(): return jax.scipy.linalg.cho_solve((factor, True), target)  31.4 us
  transfers between devices with their start and end apart: 10, of which 6 were waited for; matrix products, arithmetic and copies ran while one was open for 57% of the time, Pallas kernels for 0%

profile of v1, /device:TPU:0, one launch (start us, length us, event | category | flops | bytes accessed | tf_op | source)
XLA Modules:
  0.0 872.2 jit_solution(5936378109173707121)
XLA Ops:
  7.2 3.0 collective-permute-start
  10.3 28.9 %collective-permute-done = f32[20,128,128]{2,1,0:T(8,128)S(1)} collective-permute-done((f32[20,128,128]{2,1,0:T(8,128)}, f32[20,128,128]{2,1,0:T(8,128)S(1)}, u32[]{:S(2)}, u32[]{:S(2)}) %collective-permute-start) | collective-permute-done | bytes 1310752 | tf_op jit(solution)/shard_map/ppermute | solution.py:13
  39.2 1.5 broadcast_select_fusion.1
  40.7 1.9 collective-permute-start.1
  42.6 163.2 %multiply_reduce_fusion = f32[40,128,20,128]{3,2,1,0:T(8,128)} fusion(f32[40,1,128,20,1,128]{5,4,3,2,1,0:T(1,128)} %param.5, f32[40,20]{1,0:T(8,128)S(1)} %select_select_fusion.3), kind=kLoop, calls=%fused_computation.8 | loop fusion | flops 13107200 | bytes 104860800 | tf_op jit(solution)/shard_map/mul | solution.py:121
  205.8 1.2 select_bitcast_fusion.1
  207.0 2.6 collective-permute-start.2
  209.6 52.8 %fusion.4 = f32[5120,128]{1,0:T(8,128)S(1)} fusion(f32[2560,128]{1,0:T(8,128)S(1)} %bitcast.131, f32[640,8,20,128]{3,2,1,0:T(8,128)} %bitcast.126), kind=kOutput, calls=%fused_computation.4 | convolution fusion | flops 20132659200 | bytes 56360960 | tf_op jit(solution)/shard_map/dot_general | solution.py:80
  262.5 1.7 copy.30
  264.2 0.4 all-reduce.9.cloned.1.call-start
  264.6 2.2 convolution_bitcast_fusion.5
  266.8 34.0 %all-gather.1 = f32[1024,128]{1,0:T(8,128)S(1)} all-gather(f32[128,128]{1,0:T(8,128)S(1)} %convolution_bitcast_fusion.5), channel_id=3, replica_groups=mesh['row'=4,'col'=8] {'col'}, dimensions={0}, use_global_device_ids=true | all-gather | bytes 589824 | tf_op jit(solution)/shard_map/all_gather | solution.py:126
  301.0 2.0 maximum_select_fusion
  303.0 0.2 copy.29
  303.2 94.1 %fusion.6 = f32[2560,128]{1,0:T(8,128)S(1)} fusion(f32[5120,128]{1,0:T(8,128)S(1)} %bitcast.137, f32[640,8,20,128]{3,2,1,0:T(8,128)} %bitcast.127), kind=kOutput, calls=%fused_computation.6 | convolution fusion | flops 20132659200 | bytes 56360960 | tf_op jit(solution)/shard_map/nm,nk->mk/dot_general | solution.py:86
  397.3 2.5 bitcast_add_fusion.1
  399.9 11.7 %cholesky.70 = f32[128,128]{1,0:T(8,128)S(1)} custom-call(f32[128,128]{1,0:T(8,128)S(1)} %fusion.25), custom_call_target="Cholesky" | custom-call | tf_op jit(solution)/shard_map/jit(cholesky)/cholesky | solution.py:43
  411.7 0.6 compare_reduce_fusion.1
  412.3 0.7 fusion.15
  413.0 9.8 %custom-call.10 = f32[1,128,128]{1,2,0:T(8,128)S(1)} custom-call(f32[1,128,128]{2,1,0:T(8,128)S(1)} %fusion.15), custom_call_target="InvertDiagBlocksLowerTriangular" | custom-call | tf_op jit(solution)/shard_map/jit(_cho_solve)/triangular_solve | solution.py:44
  422.8 16.3 %all-reduce.9.cloned.1.call-done = f32[20,128,128]{2,1,0:T(8,128)} async-done(((f32[20,128,128]{2,1,0:T(8,128)}), f32[20,128,128]{2,1,0:T(8,128)}) %all-reduce.9.cloned.1.call-update) | async-done | bytes 1310736 | tf_op jit(solution)/shard_map/psum | solution.py:97
  439.1 3.5 convolution_bitcast_fusion.6
  442.6 31.7 %all-gather = f32[1024,128]{0,1:T(8,128)S(1)} all-gather(f32[128,128]{0,1:T(8,128)S(1)} %convolution_bitcast_fusion.6), channel_id=2, replica_groups=mesh['row'=4,'col'=8] {'col'}, dimensions={0}, use_global_device_ids=true | all-gather | bytes 589824 | tf_op jit(solution)/shard_map/all_gather | solution.py:126
  474.4 0.1 bitcast_reduce_fusion
  474.7 11.7 %cholesky.59 = f32[128,128]{1,0:T(8,128)S(1)} custom-call(f32[128,128]{1,0:T(8,128)S(1)} %fusion.31), custom_call_target="Cholesky" | custom-call | tf_op jit(solution)/shard_map/jit(cholesky)/cholesky | solution.py:43
  486.4 0.6 compare_reduce_fusion.2
  487.1 0.7 fusion.14
  487.7 9.8 %custom-call.9 = f32[1,128,128]{1,2,0:T(8,128)S(1)} custom-call(f32[1,128,128]{2,1,0:T(8,128)S(1)} %fusion.14), custom_call_target="InvertDiagBlocksLowerTriangular" | custom-call | tf_op jit(solution)/shard_map/jit(_cho_solve)/triangular_solve | solution.py:44
  497.5 0.3 fusion.29
  497.8 0.2 fusion.27
  498.1 2.5 convolution_subtract_fusion.1
  500.5 2.2 convolution_bitcast_fusion.4
  502.8 31.3 %all-gather.2 = f32[1024,128]{1,0:T(8,128)S(1)} all-gather(f32[128,128]{1,0:T(8,128)S(1)} %convolution_bitcast_fusion.4), channel_id=4, replica_groups=mesh['row'=4,'col'=8] {'col'}, dimensions={0}, use_global_device_ids=true | all-gather | bytes 589824 | tf_op jit(solution)/shard_map/all_gather | solution.py:126
  534.1 0.3 fusion.23
  534.4 0.2 fusion.21
  534.6 2.4 convolution_bitcast_fusion
  536.9 2.8 copy.36
  539.7 1.5 add.73
  541.2 2.0 collective-permute-start.3
  543.2 17.2 %collective-permute-done.3 = f32[20,128,128]{2,1,0:T(8,128)S(1)} collective-permute-done((f32[20,128,128]{2,1,0:T(8,128)S(1)}, f32[20,128,128]{2,1,0:T(8,128)S(1)}, u32[]{:S(2)}, u32[]{:S(2)}) %collective-permute-start.3) | collective-permute-done | bytes 1310752 | tf_op jit(solution)/shard_map/ppermute | solution.py:13
  560.4 0.2 broadcast_select_fusion
  560.7 26.5 %collective-permute-done.4 = f32[20,128,128]{2,1,0:T(8,128)S(1)} collective-permute-done((f32[20,128,128]{2,1,0:T(8,128)S(1)}, f32[20,128,128]{2,1,0:T(8,128)S(1)}, u32[]{:S(2)}, u32[]{:S(2)}) %collective-permute-start.4) | collective-permute-done | bytes 1310752 | tf_op jit(solution)/shard_map/ppermute | solution.py:13
  587.2 1.2 select_bitcast_fusion
  588.4 0.6 collective-permute-start.5
  588.9 53.3 %fusion = f32[5120,128]{1,0:T(8,128)S(1)} fusion(f32[2560,128]{1,0:T(8,128)S(1)} %bitcast.135, f32[640,8,20,128]{3,2,1,0:T(8,128)} %bitcast.128), kind=kOutput, calls=%fused_computation | convolution fusion | flops 20132659200 | bytes 56360960 | tf_op jit(solution)/shard_map/dot_general | solution.py:80
  642.2 1.7 copy.38
  644.0 3.0 maximum_select_fusion.1
  646.9 0.3 copy.37
  647.2 95.9 %fusion.2 = f32[2560,128]{1,0:T(8,128)} fusion(f32[5120,128]{1,0:T(8,128)S(1)} %bitcast.136, f32[640,8,20,128]{3,2,1,0:T(8,128)} %bitcast.129), kind=kOutput, calls=%fused_computation.2 | convolution fusion | flops 20132659200 | bytes 56360960 | tf_op jit(solution)/shard_map/nm,nk->mk/dot_general | solution.py:86
  743.1 16.5 %all-reduce.7.cloned.1.call-done = f32[20,2,128,128]{3,2,0,1:T(8,128)} async-done(((f32[20,2,128,128]{3,2,0,1:T(8,128)}), f32[20,2,128,128]{3,2,0,1:T(8,128)}) %all-reduce.7.cloned.1.call-update) | async-done | bytes 2621456 | tf_op jit(solution)/shard_map/psum | solution.py:101
  759.6 3.0 bitcast_add_fusion
  762.6 2.4 convolution_bitcast_fusion.1
  764.9 2.9 copy.33
  767.8 33.1 %all-reduce.11.cloned.1.call-done = f32[20,128,128]{2,1,0:T(8,128)} async-done(((f32[20,128,128]{2,1,0:T(8,128)}), f32[20,128,128]{2,1,0:T(8,128)}) %all-reduce.11.cloned.1.call-update) | async-done | bytes 1310736 | tf_op jit(solution)/shard_map/psum | solution.py:97
  800.9 3.5 convolution_bitcast_fusion.3
  804.4 31.5 %all-gather.3 = f32[1024,128]{1,0:T(8,128)S(1)} all-gather(f32[128,128]{1,0:T(8,128)S(1)} %convolution_bitcast_fusion.3), channel_id=5, replica_groups=mesh['row'=4,'col'=8] {'col'}, dimensions={0}, use_global_device_ids=true | all-gather | bytes 589824 | tf_op jit(solution)/shard_map/all_gather | solution.py:126
  836.0 11.7 %cholesky.81 = f32[128,128]{1,0:T(8,128)S(1)} custom-call(f32[128,128]{1,0:T(8,128)S(1)} %fusion.20), custom_call_target="Cholesky" | custom-call | tf_op jit(solution)/shard_map/jit(cholesky)/cholesky | solution.py:43
  847.8 0.6 compare_reduce_fusion
  848.4 0.7 fusion.16
  849.1 9.8 %custom-call.11 = f32[1,128,128]{1,2,0:T(8,128)S(1)} custom-call(f32[1,128,128]{2,1,0:T(8,128)S(1)} %fusion.16), custom_call_target="InvertDiagBlocksLowerTriangular" | custom-call | tf_op jit(solution)/shard_map/jit(_cho_solve)/triangular_solve | solution.py:44
  858.9 0.3 fusion.18
  859.2 0.2 convolution_bitcast_fusion.2
  859.4 3.7 fusion.12
  863.1 2.2 fusion.13
  (36 shorter events, 1.0 us)
Async XLA Ops:
  7.2 390.2 %all-reduce.5.cloned.1.call-start = ((), (), s32[]{:S(2)}) async-start(), calls=%async_computation | async-start | bytes 5242880 | tf_op jit(solution)/shard_map/psum | solution.py:101
  7.2 32.0 %collective-permute-start = (f32[20,128,128]{2,1,0:T(8,128)}, f32[20,128,128]{2,1,0:T(8,128)S(1)}, u32[]{:S(2)}, u32[]{:S(2)}) collective-permute-start(f32[20,128,128]{2,1,0:T(8,128)} %bitcast.130), channel_id=1, source_target_pairs={{0,1},{1,0},{2,3},{3,2},{4,5},{5,4},{6,7},{7,6},{8,9},{9,8},{10,11... | collective-permute-start | bytes 3932168 | tf_op jit(solution)/shard_map/ppermute | solution.py:13
  40.7 165.1 %collective-permute-start.1 = (f32[20,128,128]{2,1,0:T(8,128)S(1)}, f32[20,128,128]{2,1,0:T(8,128)}, u32[]{:S(2)}, u32[]{:S(2)}) collective-permute-start(f32[20,128,128]{2,1,0:T(8,128)S(1)} %broadcast_select_fusion.1), channel_id=1, source_target_pairs={{0,2},{1,3},{2,0},{3,1},{4,6},{5,7},{6,4},{7,5},{8,10},{9,11},{10,... | collective-permute-start | bytes 3932168 | tf_op jit(solution)/shard_map/ppermute | solution.py:13
  205.8 3.8 copy-start
  207.0 93.9 %collective-permute-start.2 = (f32[20,1,128,128]{3,2,0,1:T(8,128)}, f32[20,1,128,128]{3,2,0,1:T(8,128)S(1)}, u32[]{:S(2)}, u32[]{:S(2)}) collective-permute-start(f32[20,1,128,128]{3,2,0,1:T(8,128)} %select_bitcast_fusion.1), channel_id=1, source_target_pairs={{0,4},{1,5},{2,6},{3,7},{4,0},{5,1},{6,2},{7,3},{8,12},{9,13},{10,... | collective-permute-start | bytes 3932168 | tf_op jit(solution)/shard_map/ppermute | solution.py:13
  264.2 174.9 %all-reduce.9.cloned.1.call-start = ((), (), s32[]{:S(2)}) async-start(), calls=%async_computation.2 | async-start | bytes 2621440 | tf_op jit(solution)/shard_map/psum | solution.py:97
  399.9 359.7 %all-reduce.7.cloned.1.call-start = ((), (), s32[]{:S(2)}) async-start(), calls=%async_computation.1 | async-start | bytes 5242880 | tf_op jit(solution)/shard_map/psum | solution.py:101
  541.2 47.8 %copy-start.1 = (f32[20,128,128]{2,1,0:T(8,128)}, f32[20,128,128]{2,1,0:T(8,128)S(1)}, u32[]{:S(2)}) copy-start(f32[20,128,128]{2,1,0:T(8,128)S(1)} %add.73) | copy-start | bytes 3932164
  541.2 19.2 %collective-permute-start.3 = (f32[20,128,128]{2,1,0:T(8,128)S(1)}, f32[20,128,128]{2,1,0:T(8,128)S(1)}, u32[]{:S(2)}, u32[]{:S(2)}) collective-permute-start(f32[20,128,128]{2,1,0:T(8,128)S(1)} %add.73), channel_id=1, source_target_pairs={{0,1},{1,0},{2,3},{3,2},{4,5},{5,4},{6,7},{7,6},{8,9},{9,8},{10,11... | collective-permute-start | bytes 3932168 | tf_op jit(solution)/shard_map/ppermute | solution.py:13
  560.6 26.6 %collective-permute-start.4 = (f32[20,128,128]{2,1,0:T(8,128)S(1)}, f32[20,128,128]{2,1,0:T(8,128)S(1)}, u32[]{:S(2)}, u32[]{:S(2)}) collective-permute-start(f32[20,128,128]{2,1,0:T(8,128)S(1)} %broadcast_select_fusion), channel_id=1, source_target_pairs={{0,2},{1,3},{2,0},{3,1},{4,6},{5,7},{6,4},{7,5},{8,10},{9,11},{10,... | collective-permute-start | bytes 3932168 | tf_op jit(solution)/shard_map/ppermute | solution.py:13
  588.4 55.6 %collective-permute-start.5 = (f32[20,1,128,128]{3,2,0,1:T(8,128)}, f32[20,1,128,128]{3,2,0,1:T(8,128)}, u32[]{:S(2)}, u32[]{:S(2)}) collective-permute-start(f32[20,1,128,128]{3,2,0,1:T(8,128)} %select_bitcast_fusion), channel_id=1, source_target_pairs={{0,4},{1,5},{2,6},{3,7},{4,0},{5,1},{6,2},{7,3},{8,12},{9,13},{10,... | collective-permute-start | bytes 3932168 | tf_op jit(solution)/shard_map/ppermute | solution.py:13
  643.9 157.0 %all-reduce.11.cloned.1.call-start = ((), (), s32[]{:S(2)}) async-start(), calls=%async_computation.3 | async-start | bytes 2621440 | tf_op jit(solution)/shard_map/psum | solution.py:97
  764.9 35.9 %copy-start.2 = (f32[20,128,128]{2,1,0:T(8,128)S(1)}, f32[20,128,128]{2,1,0:T(8,128)}, u32[]{:S(2)}) copy-start(f32[20,128,128]{2,1,0:T(8,128)} %copy-done.1) | copy-start | bytes 3932164
  859.4 3.7 copy-start.3
Sparse Core Ops, SparseCore 0:
  264.3 119.9 all-reduce.4
  400.0 39.0 all-reduce.8
  644.0 115.4 all-reduce.6
  762.7 38.1 all-reduce.10
